TPU v7x, 256 devices: a whole 4x4x8 slice. The times are simulated.
256 devices in a mesh: dp: 16 (over x, y), seq: 8 (over z_hi, core), mp: 2 (over z_lo).
Axes of the slice: x: 4, y: 4, z: 8 (z_hi: 4, z_lo: 2; z = z_hi * 2 + z_lo), core: 2. Of those that a mesh axis runs over, the one named last changes fastest.
Arguments:
- hidden_states: bfloat16 [8192, 2048], P(('dp', 'seq')), may hold values from -6 to 6
- embeddings: bfloat16 [8192, 2048], P(('dp', 'seq')), may hold values from -6 to 6
- norm_gain: float32 [4096], replicated, may hold values from 0.1 to 1.9
- input_weights: bfloat16 [4096, 3, 2, 2048], P('dp', None, 'mp', 'seq'), may hold values from -0.09375 to 0.09375
- adapter_down: bfloat16 [4096, 384], P(('seq', 'mp')), may hold values from -0.09375 to 0.09375
- adapter_up: bfloat16 [3, 128, 2, 2048], P(None, None, 'mp', 'seq'), may hold values from -0.5 to 0.5
- output_weights: bfloat16 [2, 2048, 2048], P('mp', 'seq', 'dp'), may hold values from -3 to 3
- own_keys: bfloat16 [16, 8192, 4096], P('dp', 'seq', 'mp'), may hold values from -164 to 164
- own_values: bfloat16 [16, 8192, 4096], P('dp', 'seq', 'mp'), may hold values from -6 to 6
- shared_keys: bfloat16 [2, 1024, 4096], P(None, 'seq', 'mp'), may hold values from -164 to 164
- shared_values: bfloat16 [2, 1024, 4096], P(None, 'seq', 'mp'), may hold values from -6 to 6
- cached_lengths: int32 [16], P('dp'), may hold values from 1 to 8192, 65536 in all
- prompt_group: int32 [16], P('dp'), may hold values from 0 to 1
- slot_pages: int32 [16, 128], P('dp', 'seq'), may hold values from 0 to 127, as said below
- padding_mask: int32 [8192], P(('dp', 'seq', 'mp')), may hold values from 0 to 1, as said below
Outputs:
- mixed: bfloat16 [8192, 2048], P(('dp', 'seq', 'mp'))
Inputs may be any that keep to these rules, and one draw needn't show every extreme that they name: `slot_pages`: row r maps the 128 page slots of request r one to one onto its pages: slot u holds page (u + c * 16) mod 128 for a whole number c of request r; page p holds own positions p * 64 to p * 64 + 63. `padding_mask`: within each request's 512 tokens the ones come first, then the zeros; at least 128 ones.
All inputs are finite; a program needn't handle non-finite values. No bound on the sum of `cached_lengths` on one device may be relied on, other than what follows from the above.
Results may differ from a plain program's by a relative error of at most 0.025.
The roundings to bfloat16 on the way count: a program that leaves them out, or rounds other values in their place, can miss the bound.
Values may be sent and summed in bfloat16 or wider, within the bound.
A program may use at most 128 MiB of HBM per device.

v0:
```python
import math
import jax
import jax.numpy as jnp
from jax import lax
from jax.sharding import PartitionSpec as P

HD = 128
PAGE = 64
eps = 1e-05
neg_fill = -1e30
head_block = 4


def joined_2(array, axis, combine):
    everything = jax.tree.map(lambda part: lax.all_gather(part, axis), array)
    leading = jax.tree.map(lambda part: part[0], everything)

    def hop(k, so_far):
        return combine(so_far, jax.tree.map(lambda part: part[k], everything))

    return lax.fori_loop(1, lax.axis_size(axis), hop, leading)


def normalize(hidden_states, embeddings, norm_gain):
    joined = jnp.concatenate([hidden_states, embeddings], axis=1).astype(jnp.float32)
    factor = lax.rsqrt(jnp.mean(joined * joined, axis=1, keepdims=True) + eps)
    return (joined * factor * norm_gain).astype(jnp.bfloat16)


def block_partial(queries, keys, values, usable):
    head_count = queries.shape[1]
    group_size = min(head_block, head_count)
    scaling = 1.0 / math.sqrt(queries.shape[2])

    def one_group(group_index):
        offset = group_index * group_size
        query_part = lax.dynamic_slice_in_dim(queries, offset, group_size, 1)
        key_part = lax.dynamic_slice_in_dim(keys, offset, group_size, 1)
        value_part = lax.dynamic_slice_in_dim(values, offset, group_size, 1)
        scores = (
            jnp.einsum("ihd,jhd->hij", query_part, key_part, preferred_element_type=jnp.float32)
            * scaling
        )
        scores = jnp.where(usable[None], scores, neg_fill)
        peak_score = jnp.max(scores, axis=2)
        exponent = jnp.exp(scores - peak_score[:, :, None])
        totals = jnp.sum(exponent, axis=2)
        weighted = jnp.einsum(
            "hij,jhd->ihd",
            exponent.astype(jnp.bfloat16),
            value_part,
            preferred_element_type=jnp.float32,
        )
        weighted = weighted / jnp.transpose(totals)[:, :, None]
        return (weighted.astype(jnp.bfloat16), jnp.transpose(peak_score), jnp.transpose(totals))

    outputs, peak_rows, total_rows = lax.map(one_group, jnp.arange(head_count // group_size))
    row_count = queries.shape[0]
    outputs = jnp.transpose(outputs, (1, 0, 2, 3)).reshape(row_count, head_count, queries.shape[2])
    peak_rows = jnp.transpose(peak_rows, (1, 0, 2)).reshape(row_count, head_count)
    total_rows = jnp.transpose(total_rows, (1, 0, 2)).reshape(row_count, head_count)
    return (outputs, peak_rows, total_rows)


def join_partials(earlier, later):
    out_first, peak_first, total_first = earlier
    out_second, peak_second, total_second = later
    highest = jnp.maximum(peak_first, peak_second)
    weight_first = total_first * jnp.exp(peak_first - highest)
    weight_second = total_second * jnp.exp(peak_second - highest)
    summed = weight_first + weight_second
    joined = (weight_first[..., None] * out_first + weight_second[..., None] * out_second) / summed[
        ..., None
    ]
    return (joined, highest, summed)


def fold_partials(outputs, peak_scores, totals):
    highest = jnp.max(peak_scores, axis=0)
    weight = totals * jnp.exp(peak_scores - highest)
    return jnp.sum(weight[..., None] * outputs, axis=0) / jnp.sum(weight, axis=0)[..., None]


def shards(
    hidden_states,
    embeddings,
    norm_gain,
    input_weights,
    adapter_down,
    adapter_up,
    output_weights,
    own_keys,
    own_values,
    shared_keys,
    shared_values,
    cached_lengths,
    prompt_group,
    slot_pages,
    padding_mask,
):
    normed = normalize(hidden_states, embeddings, norm_gain)
    gathered = lax.all_gather(normed, "seq", axis=0, tiled=True)
    new_count = gathered.shape[0]
    columns = gathered
    low_sum = jnp.dot(
        columns,
        lax.all_gather(adapter_down, ("seq", "mp"), axis=0, tiled=True),
        preferred_element_type=jnp.float32,
    )
    low_rank = low_sum.astype(jnp.bfloat16)
    width = input_weights.shape[3]
    piece = lax.all_gather(input_weights, "dp", axis=0, tiled=True)
    columns = gathered
    base_terms = jnp.dot(
        columns, piece.reshape(piece.shape[0], 3 * width), preferred_element_type=jnp.float32
    )
    rank_size = adapter_up.shape[1]
    lifted = jnp.einsum(
        "ipr,prc->ipc",
        low_rank.reshape(new_count, 3, rank_size),
        adapter_up[:, :, 0, :],
        preferred_element_type=jnp.float32,
    )
    projected = (base_terms.reshape(new_count, 3, width) + lifted).astype(jnp.bfloat16)
    query_local = projected[:, 0]
    key_local = projected[:, 1]
    value_local = projected[:, 2]
    local_heads = width // HD
    query_all = lax.all_gather(query_local, "seq", axis=1, tiled=True)
    mp_heads = query_all.shape[1] // HD
    group_index = prompt_group[0]
    shared_k = lax.dynamic_index_in_dim(shared_keys, group_index, 0, keepdims=False)
    shared_v = lax.dynamic_index_in_dim(shared_values, group_index, 0, keepdims=False)
    slot_count = own_keys.shape[1]
    cache_keys = jnp.concatenate([own_keys[0], shared_k], axis=0).reshape(-1, mp_heads, HD)
    cache_values = jnp.concatenate([own_values[0], shared_v], axis=0).reshape(-1, mp_heads, HD)
    positions = (
        jnp.repeat(slot_pages[0], PAGE, total_repeat_length=slot_count) * PAGE
        + jnp.arange(slot_count, dtype=jnp.int32) % PAGE
    )
    usable = jnp.concatenate(
        [positions < cached_lengths[0], jnp.ones((shared_k.shape[0],), dtype=jnp.bool_)]
    )[None, :]
    cache_out, cache_peak, cache_total = block_partial(
        query_all.reshape(new_count, mp_heads, HD), cache_keys, cache_values, usable
    )
    places = jnp.arange(new_count, dtype=jnp.int32)
    causal = places[:, None] >= places[None, :]
    new_out, new_peak, new_total = block_partial(
        query_local.reshape(new_count, local_heads, HD),
        key_local.reshape(new_count, local_heads, HD),
        value_local.reshape(new_count, local_heads, HD),
        causal,
    )
    merged_out, merged_peak, merged_total = joined_2(
        (cache_out.astype(jnp.float32), cache_peak, cache_total), "seq", join_partials
    )
    first_head = lax.axis_index("seq") * local_heads
    own_out = lax.dynamic_slice_in_dim(merged_out, first_head, local_heads, 1)
    own_peak = lax.dynamic_slice_in_dim(merged_peak, first_head, local_heads, 1)
    own_total = lax.dynamic_slice_in_dim(merged_total, first_head, local_heads, 1)
    outputs = jnp.stack([own_out, new_out.astype(jnp.float32)])
    peak_scores = jnp.stack([own_peak, new_peak])
    totals = jnp.stack([own_total, new_total])
    attended = (
        fold_partials(outputs, peak_scores, totals)
        .astype(jnp.bfloat16)
        .reshape(new_count, local_heads * HD)
    )
    out_matrix = lax.all_gather(output_weights, "dp", axis=2, tiled=True)[0]
    summed = lax.psum_scatter(
        jnp.dot(attended, out_matrix, preferred_element_type=jnp.float32).astype(jnp.bfloat16),
        ("seq", "mp"),
        scatter_dimension=0,
        tiled=True,
    ).astype(jnp.float32)
    return (padding_mask.astype(jnp.float32)[:, None] * summed).astype(jnp.bfloat16)


def solution(mesh):
    placed = (
        P(("dp", "seq"), None),
        P(("dp", "seq"), None),
        P(),
        P("dp", None, "mp", "seq"),
        P(("seq", "mp"), None),
        P(None, None, "mp", "seq"),
        P("mp", "seq", "dp"),
        P("dp", "seq", "mp"),
        P("dp", "seq", "mp"),
        P(None, "seq", "mp"),
        P(None, "seq", "mp"),
        P("dp"),
        P("dp"),
        P("dp", "seq"),
        P(("dp", "seq", "mp")),
    )
    return jax.shard_map(
        shards, mesh=mesh, in_specs=placed, out_specs=P(("dp", "seq", "mp"), None), check_vma=False
    )
```

profile of v0, /device:TPU:1, one launch (start us, length us, event | category | flops | bytes accessed | tf_op | source)
XLA Modules:
  0.0 744.2 jit_solution(12947220724132167045)
XLA Ops:
  12.6 64.0 %all-gather.12.cloned.1.call-done = bf16[4096,384]{1,0:T(8,128)(2,1)} async-done(((bf16[256,384]{1,0:T(8,128)(2,1)}), bf16[4096,384]{1,0:T(8,128)(2,1)}) %all-gather.12.cloned.1.call-update) | async-done | bytes 3145744 | tf_op jit(solution)/shard_map/all_gather | solution.py:107
  76.6 54.6 %all-gather.8.cloned.1.call-done = bf16[512,4096]{1,0:T(8,128)(2,1)} async-done(((bf16[64,4096]{1,0:T(8,128)(2,1)}), bf16[512,4096]{1,0:T(8,128)(2,1)}) %all-gather.8.cloned.1.call-update) | async-done | bytes 4194320 | tf_op jit(solution)/shard_map/all_gather | solution.py:102
  131.2 5.0 convolution_convert_fusion.1
  136.2 65.8 %all-gather.10.cloned.1.call-done = bf16[4096,3,1,256]{0,3,1,2:T(8,128)(2,1)} async-done(((bf16[256,3,1,256]{0,3,1,2:T(8,128)(2,1)}), bf16[4096,3,1,256]{0,3,1,2:T(8,128)(2,1)}) %all-gather.10.cloned.1.call-update) | async-done | bytes 6291472 | tf_op jit(solution)/shard_map/all_gather | solution.py:112
  202.0 6.8 fusion.34
  213.5 6.5 copy.52
  222.0 6.4 copy.57
  229.3 4.3 compare_select_fusion.1
  233.7 5.6 fusion.58
  239.4 5.1 pad_maximum_fusion
  247.7 42.9 %while.40 = (s32[]{:T(128)}, bf16[4,512,4,128]{1,3,2,0:T(8,128)(2,1)S(1)}, f32[4,512,4]{1,2,0:T(4,128)S(1)}, f32[4,512,4]{1,2,0:T(4,128)S(1)}, s32[4]{0:T(128)S(...) while((s32[]{:T(128)}, ...), condition=%wide.region_4.5_spmd, body=%wide.region_1.0_spmd.sunk | while | flops 1234432000 | bytes 31798732 | solution.py:57
  248.9 3.2 fusion.85
  254.5 3.9 fusion.87
  265.2 3.9 fusion.87
  270.4 3.2 fusion.85
  275.9 3.9 fusion.87
  286.7 3.9 fusion.87
  293.1 5.5 copy.61
  301.5 18.6 %all_gather.30 = f32[8,512,16]{1,2,0:T(8,128)S(1)} all-gather(f32[1,512,16]{1,2,0:T(8,128)S(1)} %all_gather_reshape.6), channel_id=1, replica_groups=mesh['dp'=16,'seq'=8,'mp'=2] {'seq'}, dimensions={0}, use_global_device_ids=true | all-gather | bytes 294912 | tf_op jit(solution)/shard_map/all_gather | solution.py:15
  320.3 17.8 %all_gather.31 = f32[8,512,16]{1,2,0:T(8,128)S(1)} all-gather(f32[1,512,16]{1,2,0:T(8,128)S(1)} %all_gather_reshape.7), channel_id=1, replica_groups=mesh['dp'=16,'seq'=8,'mp'=2] {'seq'}, dimensions={0}, use_global_device_ids=true | all-gather | bytes 294912 | tf_op jit(solution)/shard_map/all_gather | solution.py:15
  338.2 261.0 %all-gather.14.cloned.1.call-done = f32[8,512,16,128]{3,2,1,0:T(8,128)} async-done(((f32[1,512,16,128]{3,2,1,0:T(8,128)}), f32[8,512,16,128]{3,2,1,0:T(8,128)}) %all-gather.14.cloned.1.call-update) | async-done | bytes 33554448 | tf_op jit(solution)/shard_map/all_gather | solution.py:15
  599.2 4.5 slice_bitcast_fusion
  603.7 66.2 %while.41 = (s32[]{:T(128)}, f32[512,16,128]{2,1,0:T(8,128)}, f32[512,16]{1,0:T(8,128)S(1)}, f32[512,16]{1,0:T(8,128)S(1)}, f32[8,512,16]{1,2,0:T(8,128)S(1)}, /...) while((s32[]{:T(128)}, f32[512,16,128]{2,1,0:T(8,128)}, ...), condition=%wide.region_6.7_spmd, body=%wide.region_5.6_spmd.sunk | while | flops 4243461 | bytes 13205655 | solution.py:21
  604.2 9.0 %fusion.89 = f32[512,16,128]{2,1,0:T(8,128)} fusion(f32[8,512,16,128]{3,2,1,0:T(8,128)} %get-tuple-element.580, s32[]{:T(128)S(6)} %select_n.128, f32[512,16,128]{2,1,0:T(8,128)} %get-tuple-element.565, f32[512,16]{1,0:T(8,128)S(1)} %get-tuple-element.577, f32[512,16]{1,0:T(8,128)S(1)} %get-tuple-element.512, f32[512,16]{1,0:T(8,128)S(1)} %get-tuple-element.513), kind=kLoop, calls=%fused_computation.23.clone.1 | loop fusion | flops 4194304 | bytes 12681220 | tf_op jit(solution)/shard_map/while/body/eval_jaxpr/div | solution.py:72
  613.7 9.0 %fusion.89 = f32[512,16,128]{2,1,0:T(8,128)} fusion(f32[8,512,16,128]{3,2,1,0:T(8,128)} %get-tuple-element.580, s32[]{:T(128)S(6)} %select_n.128, f32[512,16,128]{2,1,0:T(8,128)} %get-tuple-element.565, f32[512,16]{1,0:T(8,128)S(1)} %get-tuple-element.577, f32[512,16]{1,0:T(8,128)S(1)} %get-tuple-element.512, f32[512,16]{1,0:T(8,128)S(1)} %get-tuple-element.513), kind=kLoop, calls=%fused_computation.23.clone.1 | loop fusion | flops 4194304 | bytes 12681220 | tf_op jit(solution)/shard_map/while/body/eval_jaxpr/div | solution.py:72
  623.1 8.9 %fusion.89 = f32[512,16,128]{2,1,0:T(8,128)} fusion(f32[8,512,16,128]{3,2,1,0:T(8,128)} %get-tuple-element.580, s32[]{:T(128)S(6)} %select_n.128, f32[512,16,128]{2,1,0:T(8,128)} %get-tuple-element.565, f32[512,16]{1,0:T(8,128)S(1)} %get-tuple-element.577, f32[512,16]{1,0:T(8,128)S(1)} %get-tuple-element.512, f32[512,16]{1,0:T(8,128)S(1)} %get-tuple-element.513), kind=kLoop, calls=%fused_computation.23.clone.1 | loop fusion | flops 4194304 | bytes 12681220 | tf_op jit(solution)/shard_map/while/body/eval_jaxpr/div | solution.py:72
  632.6 9.0 %fusion.89 = f32[512,16,128]{2,1,0:T(8,128)} fusion(f32[8,512,16,128]{3,2,1,0:T(8,128)} %get-tuple-element.580, s32[]{:T(128)S(6)} %select_n.128, f32[512,16,128]{2,1,0:T(8,128)} %get-tuple-element.565, f32[512,16]{1,0:T(8,128)S(1)} %get-tuple-element.577, f32[512,16]{1,0:T(8,128)S(1)} %get-tuple-element.512, f32[512,16]{1,0:T(8,128)S(1)} %get-tuple-element.513), kind=kLoop, calls=%fused_computation.23.clone.1 | loop fusion | flops 4194304 | bytes 12681220 | tf_op jit(solution)/shard_map/while/body/eval_jaxpr/div | solution.py:72
  642.0 9.0 %fusion.89 = f32[512,16,128]{2,1,0:T(8,128)} fusion(f32[8,512,16,128]{3,2,1,0:T(8,128)} %get-tuple-element.580, s32[]{:T(128)S(6)} %select_n.128, f32[512,16,128]{2,1,0:T(8,128)} %get-tuple-element.565, f32[512,16]{1,0:T(8,128)S(1)} %get-tuple-element.577, f32[512,16]{1,0:T(8,128)S(1)} %get-tuple-element.512, f32[512,16]{1,0:T(8,128)S(1)} %get-tuple-element.513), kind=kLoop, calls=%fused_computation.23.clone.1 | loop fusion | flops 4194304 | bytes 12681220 | tf_op jit(solution)/shard_map/while/body/eval_jaxpr/div | solution.py:72
  651.5 8.9 %fusion.89 = f32[512,16,128]{2,1,0:T(8,128)} fusion(f32[8,512,16,128]{3,2,1,0:T(8,128)} %get-tuple-element.580, s32[]{:T(128)S(6)} %select_n.128, f32[512,16,128]{2,1,0:T(8,128)} %get-tuple-element.565, f32[512,16]{1,0:T(8,128)S(1)} %get-tuple-element.577, f32[512,16]{1,0:T(8,128)S(1)} %get-tuple-element.512, f32[512,16]{1,0:T(8,128)S(1)} %get-tuple-element.513), kind=kLoop, calls=%fused_computation.23.clone.1 | loop fusion | flops 4194304 | bytes 12681220 | tf_op jit(solution)/shard_map/while/body/eval_jaxpr/div | solution.py:72
  660.9 8.9 %fusion.89 = f32[512,16,128]{2,1,0:T(8,128)} fusion(f32[8,512,16,128]{3,2,1,0:T(8,128)} %get-tuple-element.580, s32[]{:T(128)S(6)} %select_n.128, f32[512,16,128]{2,1,0:T(8,128)} %get-tuple-element.565, f32[512,16]{1,0:T(8,128)S(1)} %get-tuple-element.577, f32[512,16]{1,0:T(8,128)S(1)} %get-tuple-element.512, f32[512,16]{1,0:T(8,128)S(1)} %get-tuple-element.513), kind=kLoop, calls=%fused_computation.23.clone.1 | loop fusion | flops 4194304 | bytes 12681220 | tf_op jit(solution)/shard_map/while/body/eval_jaxpr/div | solution.py:72
  672.5 3.3 convolution_convert_fusion
  675.9 59.8 %reduce-scatter.2.cloned.1.call-done = bf16[32,2048]{1,0:T(8,128)(2,1)} async-done(((bf16[512,2048]{1,0:T(8,128)(2,1)}), bf16[32,2048]{1,0:T(8,128)(2,1)}) %reduce-scatter.2.cloned.1.call-update) | async-done | bytes 131088 | tf_op jit(solution)/shard_map/reduce_scatter | solution.py:171
  (117 shorter events, 46.9 us)
Async XLA Ops:
  6.5 202.3 %copy-start = (bf16[3,128,1,256]{3,1,2,0:T(8,128)(2,1)S(1)}, bf16[3,128,1,256]{3,1,2,0:T(8,128)(2,1)}, u32[]{:S(2)}) copy-start(bf16[3,128,1,256]{3,1,2,0:T(8,128)(2,1)} %param.26) | copy-start | bytes 589828
  6.5 70.1 %all-gather.12.cloned.1.call-start = ((), (), s32[]{:S(2)}) async-start(), calls=%async_computation.3 | async-start | bytes 3342336 | tf_op jit(solution)/shard_map/all_gather | solution.py:107
  7.3 124.0 %all-gather.8.cloned.1.call-start = ((), (), s32[]{:S(2)}) async-start(), calls=%async_computation.1 | async-start | bytes 4718592 | tf_op jit(solution)/shard_map/all_gather | solution.py:102
  10.6 191.4 %all-gather.10.cloned.1.call-start = ((), (), s32[]{:S(2)}) async-start(), calls=%async_computation.2 | async-start | bytes 6684672 | tf_op jit(solution)/shard_map/all_gather | solution.py:112
  12.6 235.1 %all-gather.18.cloned.1.call-start = ((), (), s32[]{:S(2)}) async-start(), calls=%async_computation.7 | async-start | bytes 2359296 | tf_op jit(solution)/shard_map/all_gather | solution.py:129
  210.2 389.0 %all-gather.14.cloned.1.call-start = ((), (), s32[]{:S(2)}) async-start(), calls=%async_computation.4 | async-start | bytes 37748736 | tf_op jit(solution)/shard_map/all_gather | solution.py:15
  222.0 6.5 copy-start.6
  222.0 7.2 copy-start.7
  239.4 5.1 copy-start.2
  298.6 0.9 copy-start.3
  298.6 1.0 copy-start.4
  298.6 2.2 copy-start.5
  298.6 373.9 %all-gather.16.cloned.1.call-start = ((), (), s32[]{:S(2)}) async-start(), calls=%async_computation.5 | async-start | bytes 1114112 | tf_op jit(solution)/shard_map/all_gather | solution.py:170
  299.2 436.5 %reduce-scatter.2.cloned.1.call-start = ((), (), s32[]{:S(2)}) async-start(), calls=%async_computation.6 | async-start | bytes 2228224 | tf_op jit(solution)/shard_map/reduce_scatter | solution.py:171
  672.3 3.6 copy-start.8
  672.3 65.1 %copy-start.1 = (bf16[3,128,1,256]{3,1,2,0:T(8,128)(2,1)S(1)}, bf16[3,128,1,256]{3,1,2,0:T(8,128)(2,1)}, u32[]{:S(2)}) copy-start(bf16[3,128,1,256]{3,1,2,0:T(8,128)(2,1)} %param.26) | copy-start | bytes 589828
Sparse Core Ops, SparseCore 0:
  9.1 67.4 all-gather.11
  78.5 52.7 all-gather.7
  133.7 68.3 all-gather.9
  210.3 37.3 all-gather.17
  298.7 300.4 all-gather.13
  601.5 44.6 all-gather.15
  676.0 59.6 reduce-scatter.1
where the time goes:
time: 747 us; the launch traced here: 744 us
  waiting for transfers between devices  507 us (68%)
  other arithmetic  99.7 us (13%)
  matrix products  45.5 us (6%)
  local copies, waits for them, and re-layouts  37.5 us (5%)
  blocking collectives  36.4 us (5%)
  between operations  15.1 us (2%)
    all_gather x1, waiting for transfers between devices, joined_2(): everything = jax.tree.map(lambda part: lax.all_gather(part, axis), array)  261 us
    all_gather x1, waiting for transfers between devices, shards(): piece = lax.all_gather(input_weights, 'dp', axis=0, tiled=True)  65.8 us
    all_gather x1, waiting for transfers between devices, shards(): lax.all_gather(adapter_down, ('seq', 'mp'), axis=0, tiled=True)  64 us
    div x7, other arithmetic, join_partials(): (weight_first[..., None] * out_first + weight_second[..., None] * out_sec...  62.7 us
    reduce_scatter x1, waiting for transfers between devices, shards(): lax.psum_scatter(jnp.dot(attended, out_matrix, preferred_element_type=jnp...  59.8 us
    all_gather x1, waiting for transfers between devices, shards(): gathered = lax.all_gather(normed, 'seq', axis=0, tiled=True)  54.6 us
    all_gather x2, blocking collectives, joined_2(): everything = jax.tree.map(lambda part: lax.all_gather(part, axis), array)  36.4 us
    unnamed x22, local copies, waits for them, and re-layouts  16.5 us
  transfers between devices with their start and end apart: 7, of which 6 were waited for; matrix products, arithmetic and copies ran while one was open for 16% of the time, Pallas kernels for 0%

commit v1 on v0

--- a/solution.py
+++ b/solution.py
@@ -9,6 +9,27 @@
 eps = 1e-05
 neg_fill = -1e30
 head_block = 4
+
+
+def gather_around(x, axis, dim):
+    size, index, rows = (lax.axis_size(axis), lax.axis_index(axis), x.shape[dim])
+    right = [(i, (i + 1) % size) for i in range(size)]
+    left = [(i, (i - 1) % size) for i in range(size)]
+    filled = jnp.zeros((*x.shape[:dim], size * rows, *x.shape[dim + 1 :]), x.dtype)
+    filled = lax.dynamic_update_slice_in_dim(filled, x, index * rows, axis=dim)
+    from_left = from_right = x
+    middle = size // 2
+    for hop in range(1, middle + 1):
+        from_left = lax.ppermute(from_left, axis, right)
+        filled = lax.dynamic_update_slice_in_dim(
+            filled, from_left, (index - hop) % size * rows, axis=dim
+        )
+        if hop < size - middle:
+            from_right = lax.ppermute(from_right, axis, left)
+            filled = lax.dynamic_update_slice_in_dim(
+                filled, from_right, (index + hop) % size * rows, axis=dim
+            )
+    return filled
 
 
 def joined_2(array, axis, combine):
@@ -109,7 +130,7 @@
     )
     low_rank = low_sum.astype(jnp.bfloat16)
     width = input_weights.shape[3]
-    piece = lax.all_gather(input_weights, "dp", axis=0, tiled=True)
+    piece = gather_around(input_weights, "dp", 0)
     columns = gathered
     base_terms = jnp.dot(
         columns, piece.reshape(piece.shape[0], 3 * width), preferred_element_type=jnp.float32

time: 747 us -> 679 us (0.909)
  waiting for transfers between devices: 507 us -> 390 us
  starting transfers between devices: 0.43 us -> 35.9 us
  local copies, waits for them, and re-layouts: 37.5 us -> 53.5 us
    all_gather x1 -> x0, waiting for transfers between devices: 65.8 us -> none  [shards(): piece = lax.all_gather(input_weights, 'dp', axis=0, tiled=True)]
    all_gather x1, waiting for transfers between devices: 64 us -> 0.01 us  [shards(): lax.all_gather(adapter_down, ('seq', 'mp'), axis=0, tiled=True)]
    ppermute x0 -> x15, waiting for transfers between devices: none -> 36.7 us  [the longest x8 29.3 us: gather_around(): from_left = lax.ppermute(from_left, axis, right)]
    ppermute x0 -> x15, starting transfers between devices: none -> 35.5 us  [the longest x7 33.3 us: gather_around(): from_right = lax.ppermute(from_right, axis, left)]
    all_gather x1, waiting for transfers between devices: 54.6 us -> 30.3 us  [shards(): gathered = lax.all_gather(normed, 'seq', axis=0, tiled=True)]
    dynamic_update_slice x0 -> x16, local copies, waits for them, and re-layouts: none -> 13.3 us  [the longest x8 6.68 us: gather_around(): lax.dynamic_update_slice_in_dim(filled, from_left, (index - hop) % size *...]
    unnamed x22 -> x32, local copies, waits for them, and re-layouts: 16.5 us -> 15.5 us
  transfers between devices with their start and end apart: 7 -> 21, of which waited for: 6 -> 13; matrix products, arithmetic and copies ran while one was open for 16% -> 20% of each run, Pallas kernels for 0% -> 0%
where the time goes in v1:
time: 679 us; the launch traced here: 676 us
  waiting for transfers between devices  390 us (57%)
  other arithmetic  99.8 us (15%)
  local copies, waits for them, and re-layouts  53.5 us (8%)
  matrix products  45 us (7%)
  starting transfers between devices  35.9 us (5%)
  blocking collectives  34.3 us (5%)
  between operations  15.1 us (2%)
    all_gather x1, waiting for transfers between devices, joined_2(): everything = jax.tree.map(lambda part: lax.all_gather(part, axis), array)  261 us
    div x7, other arithmetic, join_partials(): (weight_first[..., None] * out_first + weight_second[..., None] * out_sec...  62.7 us
    reduce_scatter x1, waiting for transfers between devices, shards(): lax.psum_scatter(jnp.dot(attended, out_matrix, preferred_element_type=jnp...  60.9 us
    all_gather x2, blocking collectives, joined_2(): everything = jax.tree.map(lambda part: lax.all_gather(part, axis), array)  34.3 us
    ppermute x7, starting transfers between devices, gather_around(): from_right = lax.ppermute(from_right, axis, left)  33.3 us
    all_gather x1, waiting for transfers between devices, shards(): gathered = lax.all_gather(normed, 'seq', axis=0, tiled=True)  30.3 us
    ppermute x8, waiting for transfers between devices, gather_around(): from_left = lax.ppermute(from_left, axis, right)  29.3 us
    dot_general x5, matrix products, one_group(): jnp.einsum('hij,jhd->ihd', exponent.astype(jnp.bfloat16), value_part, pre...  16.3 us
  transfers between devices with their start and end apart: 21, of which 13 were waited for; matrix products, arithmetic and copies ran while one was open for 20% of the time, Pallas kernels for 0%

profile of v1, /device:TPU:1, one launch (start us, length us, event | category | flops | bytes accessed | tf_op | source)
XLA Modules:
  0.0 676.4 jit_solution(120031966836470432)
XLA Ops:
  17.8 6.9 %collective-permute-done = bf16[256,3,1,256]{0,3,1,2:T(8,128)(2,1)S(1)} collective-permute-done((bf16[256,3,1,256]{0,3,1,2:T(8,128)(2,1)S(1)}, bf16[256,3,1,256]{0,3,1,2:T(8,128)(2,1)S(1)}, u32[]{:S(2)}, u32[]{:S(2)}) %collective-permute-start) | collective-permute-done | bytes 393248 | tf_op jit(solution)/shard_map/ppermute | solution.py:23
  24.7 4.8 collective-permute-start.3
  29.4 6.1 collective-permute-done.2
  35.6 4.8 collective-permute-start.5
  40.3 5.2 collective-permute-done.4
  45.5 4.8 collective-permute-start.7
  50.3 5.2 collective-permute-done.6
  60.6 4.8 collective-permute-start.9
  70.1 5.2 collective-permute-start.11
  81.3 5.2 collective-permute-start.13
  94.5 5.6 collective-permute-done.14
  100.9 30.3 %all-gather.7.cloned.1.call-done = bf16[512,4096]{1,0:T(8,128)(2,1)} async-done(((bf16[64,4096]{1,0:T(8,128)(2,1)}), bf16[512,4096]{1,0:T(8,128)(2,1)}) %all-gather.7.cloned.1.call-update) | async-done | bytes 4194320 | tf_op jit(solution)/shard_map/all_gather | solution.py:123
  131.2 5.1 convolution_convert_fusion.1
  136.8 6.2 fusion.40
  147.3 6.5 copy.54
  155.9 6.4 copy.61
  167.7 5.6 fusion.63
  173.3 5.1 pad_maximum_fusion
  181.3 43.2 %while.40 = (s32[]{:T(128)}, bf16[4,512,4,128]{1,3,2,0:T(8,128)(2,1)S(1)}, f32[4,512,4]{1,2,0:T(4,128)S(1)}, f32[4,512,4]{1,2,0:T(4,128)S(1)}, s32[4]{0:T(128)S(...) while((s32[]{:T(128)}, ...), condition=%wide.region_4.5_spmd, body=%wide.region_1.4_spmd.sunk | while | flops 1234432000 | bytes 31798732 | solution.py:78
  227.0 5.5 copy.65
  235.2 14.8 %all_gather.26 = f32[8,512,16]{1,2,0:T(8,128)S(1)} all-gather(f32[1,512,16]{1,2,0:T(8,128)S(1)} %all_gather_reshape.6), channel_id=1, replica_groups=mesh['dp'=16,'seq'=8,'mp'=2] {'seq'}, dimensions={0}, use_global_device_ids=true | all-gather | bytes 294912 | tf_op jit(solution)/shard_map/all_gather | solution.py:36
  250.2 19.5 %all_gather.27 = f32[8,512,16]{1,2,0:T(8,128)S(1)} all-gather(f32[1,512,16]{1,2,0:T(8,128)S(1)} %all_gather_reshape.7), channel_id=1, replica_groups=mesh['dp'=16,'seq'=8,'mp'=2] {'seq'}, dimensions={0}, use_global_device_ids=true | all-gather | bytes 294912 | tf_op jit(solution)/shard_map/all_gather | solution.py:36
  269.9 260.6 %all-gather.11.cloned.1.call-done = f32[8,512,16,128]{3,2,1,0:T(8,128)} async-done(((f32[1,512,16,128]{3,2,1,0:T(8,128)}), f32[8,512,16,128]{3,2,1,0:T(8,128)}) %all-gather.11.cloned.1.call-update) | async-done | bytes 33554448 | tf_op jit(solution)/shard_map/all_gather | solution.py:36
  534.9 66.1 %while.41 = (s32[]{:T(128)}, f32[512,16,128]{2,1,0:T(8,128)}, f32[512,16]{1,0:T(8,128)S(1)}, f32[512,16]{1,0:T(8,128)S(1)}, f32[8,512,16]{1,2,0:T(8,128)S(1)}, /...) while((s32[]{:T(128)}, f32[512,16,128]{2,1,0:T(8,128)}, ...), condition=%wide.region_6.7_spmd, body=%wide.region_5.6_spmd.sunk | while | flops 4243461 | bytes 13205655 | solution.py:42
  535.4 8.9 %fusion.95 = f32[512,16,128]{2,1,0:T(8,128)} fusion(f32[8,512,16,128]{3,2,1,0:T(8,128)} %get-tuple-element.580, s32[]{:T(128)S(6)} %select_n.269, f32[512,16,128]{2,1,0:T(8,128)} %get-tuple-element.565, f32[512,16]{1,0:T(8,128)S(1)} %get-tuple-element.577, f32[512,16]{1,0:T(8,128)S(1)} %get-tuple-element.512, f32[512,16]{1,0:T(8,128)S(1)} %get-tuple-element.513), kind=kLoop, calls=%fused_computation.23.clone.1 | loop fusion | flops 4194304 | bytes 12681220 | tf_op jit(solution)/shard_map/while/body/eval_jaxpr/div | solution.py:93
  544.9 8.9 %fusion.95 = f32[512,16,128]{2,1,0:T(8,128)} fusion(f32[8,512,16,128]{3,2,1,0:T(8,128)} %get-tuple-element.580, s32[]{:T(128)S(6)} %select_n.269, f32[512,16,128]{2,1,0:T(8,128)} %get-tuple-element.565, f32[512,16]{1,0:T(8,128)S(1)} %get-tuple-element.577, f32[512,16]{1,0:T(8,128)S(1)} %get-tuple-element.512, f32[512,16]{1,0:T(8,128)S(1)} %get-tuple-element.513), kind=kLoop, calls=%fused_computation.23.clone.1 | loop fusion | flops 4194304 | bytes 12681220 | tf_op jit(solution)/shard_map/while/body/eval_jaxpr/div | solution.py:93
  554.3 8.9 %fusion.95 = f32[512,16,128]{2,1,0:T(8,128)} fusion(f32[8,512,16,128]{3,2,1,0:T(8,128)} %get-tuple-element.580, s32[]{:T(128)S(6)} %select_n.269, f32[512,16,128]{2,1,0:T(8,128)} %get-tuple-element.565, f32[512,16]{1,0:T(8,128)S(1)} %get-tuple-element.577, f32[512,16]{1,0:T(8,128)S(1)} %get-tuple-element.512, f32[512,16]{1,0:T(8,128)S(1)} %get-tuple-element.513), kind=kLoop, calls=%fused_computation.23.clone.1 | loop fusion | flops 4194304 | bytes 12681220 | tf_op jit(solution)/shard_map/while/body/eval_jaxpr/div | solution.py:93
  563.7 9.0 %fusion.95 = f32[512,16,128]{2,1,0:T(8,128)} fusion(f32[8,512,16,128]{3,2,1,0:T(8,128)} %get-tuple-element.580, s32[]{:T(128)S(6)} %select_n.269, f32[512,16,128]{2,1,0:T(8,128)} %get-tuple-element.565, f32[512,16]{1,0:T(8,128)S(1)} %get-tuple-element.577, f32[512,16]{1,0:T(8,128)S(1)} %get-tuple-element.512, f32[512,16]{1,0:T(8,128)S(1)} %get-tuple-element.513), kind=kLoop, calls=%fused_computation.23.clone.1 | loop fusion | flops 4194304 | bytes 12681220 | tf_op jit(solution)/shard_map/while/body/eval_jaxpr/div | solution.py:93
  573.2 9.0 %fusion.95 = f32[512,16,128]{2,1,0:T(8,128)} fusion(f32[8,512,16,128]{3,2,1,0:T(8,128)} %get-tuple-element.580, s32[]{:T(128)S(6)} %select_n.269, f32[512,16,128]{2,1,0:T(8,128)} %get-tuple-element.565, f32[512,16]{1,0:T(8,128)S(1)} %get-tuple-element.577, f32[512,16]{1,0:T(8,128)S(1)} %get-tuple-element.512, f32[512,16]{1,0:T(8,128)S(1)} %get-tuple-element.513), kind=kLoop, calls=%fused_computation.23.clone.1 | loop fusion | flops 4194304 | bytes 12681220 | tf_op jit(solution)/shard_map/while/body/eval_jaxpr/div | solution.py:93
  582.7 8.9 %fusion.95 = f32[512,16,128]{2,1,0:T(8,128)} fusion(f32[8,512,16,128]{3,2,1,0:T(8,128)} %get-tuple-element.580, s32[]{:T(128)S(6)} %select_n.269, f32[512,16,128]{2,1,0:T(8,128)} %get-tuple-element.565, f32[512,16]{1,0:T(8,128)S(1)} %get-tuple-element.577, f32[512,16]{1,0:T(8,128)S(1)} %get-tuple-element.512, f32[512,16]{1,0:T(8,128)S(1)} %get-tuple-element.513), kind=kLoop, calls=%fused_computation.23.clone.1 | loop fusion | flops 4194304 | bytes 12681220 | tf_op jit(solution)/shard_map/while/body/eval_jaxpr/div | solution.py:93
  592.1 8.9 %fusion.95 = f32[512,16,128]{2,1,0:T(8,128)} fusion(f32[8,512,16,128]{3,2,1,0:T(8,128)} %get-tuple-element.580, s32[]{:T(128)S(6)} %select_n.269, f32[512,16,128]{2,1,0:T(8,128)} %get-tuple-element.565, f32[512,16]{1,0:T(8,128)S(1)} %get-tuple-element.577, f32[512,16]{1,0:T(8,128)S(1)} %get-tuple-element.512, f32[512,16]{1,0:T(8,128)S(1)} %get-tuple-element.513), kind=kLoop, calls=%fused_computation.23.clone.1 | loop fusion | flops 4194304 | bytes 12681220 | tf_op jit(solution)/shard_map/while/body/eval_jaxpr/div | solution.py:93
  607.1 60.9 %reduce-scatter.2.cloned.1.call-done = bf16[32,2048]{1,0:T(8,128)(2,1)} async-done(((bf16[512,2048]{1,0:T(8,128)(2,1)}), bf16[32,2048]{1,0:T(8,128)(2,1)}) %reduce-scatter.2.cloned.1.call-update) | async-done | bytes 131088 | tf_op jit(solution)/shard_map/reduce_scatter | solution.py:192
  (171 shorter events, 110.5 us)
Async XLA Ops:
  6.5 129.8 %copy-start = (bf16[3,128,1,256]{3,1,2,0:T(8,128)(2,1)S(1)}, bf16[3,128,1,256]{3,1,2,0:T(8,128)(2,1)}, u32[]{:S(2)}) copy-start(bf16[3,128,1,256]{3,1,2,0:T(8,128)(2,1)} %param.26) | copy-start | bytes 589828
  6.5 94.4 %all-gather.9.cloned.1.call-start = ((), (), s32[]{:S(2)}) async-start(), calls=%async_computation.2 | async-start | bytes 3342336 | tf_op jit(solution)/shard_map/all_gather | solution.py:128
  7.3 124.0 %all-gather.7.cloned.1.call-start = ((), (), s32[]{:S(2)}) async-start(), calls=%async_computation.1 | async-start | bytes 4718592 | tf_op jit(solution)/shard_map/all_gather | solution.py:123
  10.6 170.7 %all-gather.15.cloned.1.call-start = ((), (), s32[]{:S(2)}) async-start(), calls=%async_computation.6 | async-start | bytes 2359296 | tf_op jit(solution)/shard_map/all_gather | solution.py:150
  11.9 12.8 %collective-permute-start = (bf16[256,3,1,256]{0,3,1,2:T(8,128)(2,1)S(1)}, bf16[256,3,1,256]{0,3,1,2:T(8,128)(2,1)S(1)}, u32[]{:S(2)}, u32[]{:S(2)}) collective-permute-start(bf16[256,3,1,256]{0,3,1,2:T(8,128)(2,1)S(1)} %copy.56), channel_id=1, source_target_pairs={{0,16},{16,32},{32,48},{48,64},{64,80},{80,96},{96,112},{112,128},... | collective-permute-start | bytes 1179656 | tf_op jit(solution)/shard_map/ppermute | solution.py:23
  14.0 10.6 %collective-permute-start.1 = (bf16[256,3,1,256]{0,3,1,2:T(8,128)(2,1)S(1)}, bf16[256,3,1,256]{0,3,1,2:T(8,128)(2,1)S(1)}, u32[]{:S(2)}, u32[]{:S(2)}) collective-permute-start(bf16[256,3,1,256]{0,3,1,2:T(8,128)(2,1)S(1)} %copy.56), channel_id=1, source_target_pairs={{0,240},{16,0},{32,16},{48,32},{64,48},{80,64},{96,80},{112,96},{1... | collective-permute-start | bytes 1179656 | tf_op jit(solution)/shard_map/ppermute | solution.py:28
  24.7 15.7 %copy-start.7 = (bf16[256,3,1,256]{0,3,1,2:T(8,128)(2,1)}, bf16[256,3,1,256]{0,3,1,2:T(8,128)(2,1)S(1)}, u32[]{:S(2)}) copy-start(bf16[256,3,1,256]{0,3,1,2:T(8,128)(2,1)S(1)} %collective-permute-done) | copy-start | bytes 1179652
  24.7 10.9 %collective-permute-start.2 = (bf16[256,3,1,256]{0,3,1,2:T(8,128)(2,1)S(1)}, bf16[256,3,1,256]{0,3,1,2:T(8,128)(2,1)S(1)}, u32[]{:S(2)}, u32[]{:S(2)}) collective-permute-start(bf16[256,3,1,256]{0,3,1,2:T(8,128)(2,1)S(1)} %collective-permute-done), channel_id=1, source_target_pairs={{0,16},{16,32},{32,48},{48,64},{64,80},{80,96},{96,112},{112,128},... | collective-permute-start | bytes 1179656 | tf_op jit(solution)/shard_map/ppermute | solution.py:23
  24.7 10.9 %collective-permute-start.3 = (bf16[256,3,1,256]{0,3,1,2:T(8,128)(2,1)S(1)}, bf16[256,3,1,256]{0,3,1,2:T(8,128)(2,1)S(1)}, u32[]{:S(2)}, u32[]{:S(2)}) collective-permute-start(bf16[256,3,1,256]{0,3,1,2:T(8,128)(2,1)S(1)} %collective-permute-done.1), channel_id=1, source_target_pairs={{0,240},{16,0},{32,16},{48,32},{64,48},{80,64},{96,80},{112,96},{1... | collective-permute-start | bytes 1179656 | tf_op jit(solution)/shard_map/ppermute | solution.py:28
  35.6 9.9 %collective-permute-start.4 = (bf16[256,3,1,256]{0,3,1,2:T(8,128)(2,1)S(1)}, bf16[256,3,1,256]{0,3,1,2:T(8,128)(2,1)S(1)}, u32[]{:S(2)}, u32[]{:S(2)}) collective-permute-start(bf16[256,3,1,256]{0,3,1,2:T(8,128)(2,1)S(1)} %collective-permute-done.2), channel_id=1, source_target_pairs={{0,16},{16,32},{32,48},{48,64},{64,80},{80,96},{96,112},{112,128},... | collective-permute-start | bytes 1179656 | tf_op jit(solution)/shard_map/ppermute | solution.py:23
  35.6 9.9 %collective-permute-start.5 = (bf16[256,3,1,256]{0,3,1,2:T(8,128)(2,1)S(1)}, bf16[256,3,1,256]{0,3,1,2:T(8,128)(2,1)S(1)}, u32[]{:S(2)}, u32[]{:S(2)}) collective-permute-start(bf16[256,3,1,256]{0,3,1,2:T(8,128)(2,1)S(1)} %collective-permute-done.3), channel_id=1, source_target_pairs={{0,240},{16,0},{32,16},{48,32},{64,48},{80,64},{96,80},{112,96},{1... | collective-permute-start | bytes 1179656 | tf_op jit(solution)/shard_map/ppermute | solution.py:28
  45.5 10.0 %copy-start.5 = (bf16[256,3,1,256]{0,3,1,2:T(8,128)(2,1)}, bf16[256,3,1,256]{0,3,1,2:T(8,128)(2,1)S(1)}, u32[]{:S(2)}) copy-start(bf16[256,3,1,256]{0,3,1,2:T(8,128)(2,1)S(1)} %collective-permute-done.4) | copy-start | bytes 1179652
  45.5 9.9 %collective-permute-start.6 = (bf16[256,3,1,256]{0,3,1,2:T(8,128)(2,1)S(1)}, bf16[256,3,1,256]{0,3,1,2:T(8,128)(2,1)S(1)}, u32[]{:S(2)}, u32[]{:S(2)}) collective-permute-start(bf16[256,3,1,256]{0,3,1,2:T(8,128)(2,1)S(1)} %collective-permute-done.4), channel_id=1, source_target_pairs={{0,16},{16,32},{32,48},{48,64},{64,80},{80,96},{96,112},{112,128},... | collective-permute-start | bytes 1179656 | tf_op jit(solution)/shard_map/ppermute | solution.py:23
  45.5 15.1 %collective-permute-start.7 = (bf16[256,3,1,256]{0,3,1,2:T(8,128)(2,1)S(1)}, bf16[256,3,1,256]{0,3,1,2:T(8,128)(2,1)S(1)}, u32[]{:S(2)}, u32[]{:S(2)}) collective-permute-start(bf16[256,3,1,256]{0,3,1,2:T(8,128)(2,1)S(1)} %collective-permute-done.5), channel_id=1, source_target_pairs={{0,240},{16,0},{32,16},{48,32},{64,48},{80,64},{96,80},{112,96},{1... | collective-permute-start | bytes 1179656 | tf_op jit(solution)/shard_map/ppermute | solution.py:28
  55.5 10.7 %collective-permute-start.8 = (bf16[256,3,1,256]{0,3,1,2:T(8,128)(2,1)S(1)}, bf16[256,3,1,256]{0,3,1,2:T(8,128)(2,1)S(1)}, u32[]{:S(2)}, u32[]{:S(2)}) collective-permute-start(bf16[256,3,1,256]{0,3,1,2:T(8,128)(2,1)S(1)} %collective-permute-done.6), channel_id=1, source_target_pairs={{0,16},{16,32},{32,48},{48,64},{64,80},{80,96},{96,112},{112,128},... | collective-permute-start | bytes 1179656 | tf_op jit(solution)/shard_map/ppermute | solution.py:23
  55.5 12.4 %copy-start.6 = (bf16[256,3,1,256]{0,3,1,2:T(8,128)(2,1)S(1)}, bf16[256,3,1,256]{0,3,1,2:T(8,128)(2,1)}, u32[]{:S(2)}) copy-start(bf16[256,3,1,256]{0,3,1,2:T(8,128)(2,1)} %copy-done.5) | copy-start | bytes 1179652
  60.6 9.5 %collective-permute-start.9 = (bf16[256,3,1,256]{0,3,1,2:T(8,128)(2,1)S(1)}, bf16[256,3,1,256]{0,3,1,2:T(8,128)(2,1)S(1)}, u32[]{:S(2)}, u32[]{:S(2)}) collective-permute-start(bf16[256,3,1,256]{0,3,1,2:T(8,128)(2,1)S(1)} %collective-permute-done.7), channel_id=1, source_target_pairs={{0,240},{16,0},{32,16},{48,32},{64,48},{80,64},{96,80},{112,96},{1... | collective-permute-start | bytes 1179656 | tf_op jit(solution)/shard_map/ppermute | solution.py:28
  66.2 10.1 %collective-permute-start.10 = (bf16[256,3,1,256]{0,3,1,2:T(8,128)(2,1)S(1)}, bf16[256,3,1,256]{0,3,1,2:T(8,128)(2,1)S(1)}, u32[]{:S(2)}, u32[]{:S(2)}) collective-permute-start(bf16[256,3,1,256]{0,3,1,2:T(8,128)(2,1)S(1)} %collective-permute-done.8), channel_id=1, source_target_pairs={{0,16},{16,32},{32,48},{48,64},{64,80},{80,96},{96,112},{112,128},... | collective-permute-start | bytes 1179656 | tf_op jit(solution)/shard_map/ppermute | solution.py:23
  70.1 11.2 %collective-permute-start.11 = (bf16[256,3,1,256]{0,3,1,2:T(8,128)(2,1)S(1)}, bf16[256,3,1,256]{0,3,1,2:T(8,128)(2,1)S(1)}, u32[]{:S(2)}, u32[]{:S(2)}) collective-permute-start(bf16[256,3,1,256]{0,3,1,2:T(8,128)(2,1)S(1)} %collective-permute-done.9), channel_id=1, source_target_pairs={{0,240},{16,0},{32,16},{48,32},{64,48},{80,64},{96,80},{112,96},{1... | collective-permute-start | bytes 1179656 | tf_op jit(solution)/shard_map/ppermute | solution.py:28
  76.3 11.3 %collective-permute-start.12 = (bf16[256,3,1,256]{0,3,1,2:T(8,128)(2,1)S(1)}, bf16[256,3,1,256]{0,3,1,2:T(8,128)(2,1)S(1)}, u32[]{:S(2)}, u32[]{:S(2)}) collective-permute-start(bf16[256,3,1,256]{0,3,1,2:T(8,128)(2,1)S(1)} %collective-permute-done.10), channel_id=1, source_target_pairs={{0,16},{16,32},{32,48},{48,64},{64,80},{80,96},{96,112},{112,128},... | collective-permute-start | bytes 1179656 | tf_op jit(solution)/shard_map/ppermute | solution.py:23
  81.3 12.3 %collective-permute-start.13 = (bf16[256,3,1,256]{0,3,1,2:T(8,128)(2,1)S(1)}, bf16[256,3,1,256]{0,3,1,2:T(8,128)(2,1)S(1)}, u32[]{:S(2)}, u32[]{:S(2)}) collective-permute-start(bf16[256,3,1,256]{0,3,1,2:T(8,128)(2,1)S(1)} %collective-permute-done.11), channel_id=1, source_target_pairs={{0,240},{16,0},{32,16},{48,32},{64,48},{80,64},{96,80},{112,96},{1... | collective-permute-start | bytes 1179656 | tf_op jit(solution)/shard_map/ppermute | solution.py:28
  87.6 12.5 %collective-permute-start.14 = (bf16[256,3,1,256]{0,3,1,2:T(8,128)(2,1)S(1)}, bf16[256,3,1,256]{0,3,1,2:T(8,128)(2,1)S(1)}, u32[]{:S(2)}, u32[]{:S(2)}) collective-permute-start(bf16[256,3,1,256]{0,3,1,2:T(8,128)(2,1)S(1)} %collective-permute-done.12), channel_id=1, source_target_pairs={{0,16},{16,32},{32,48},{48,64},{64,80},{80,96},{96,112},{112,128},... | collective-permute-start | bytes 1179656 | tf_op jit(solution)/shard_map/ppermute | solution.py:23
  131.2 5.6 copy-start.12
  144.0 386.5 %all-gather.11.cloned.1.call-start = ((), (), s32[]{:S(2)}) async-start(), calls=%async_computation.3 | async-start | bytes 37748736 | tf_op jit(solution)/shard_map/all_gather | solution.py:36
  154.4 7.9 %copy-start.10 = (s32[1,16]{1,0:T(1,128)S(1)}, s32[1,16]{1,0:T(1,128)}, u32[]{:S(2)}) copy-start(s32[1,16]{1,0:T(1,128)} %param.34) | copy-start | bytes 196
  154.5 8.6 %copy-start.11 = (s32[8,128]{1,0:T(8,128)S(1)}, s32[8,128]{1,0:T(8,128)}, u32[]{:S(2)}) copy-start(s32[8,128]{1,0:T(8,128)} %constant.310.clone.1) | copy-start | bytes 12292
  173.3 5.1 copy-start.2
  227.0 6.3 copy-start.3
  227.0 6.3 copy-start.4
  232.6 371.1 %all-gather.13.cloned.1.call-start = ((), (), s32[]{:S(2)}) async-start(), calls=%async_computation.4 | async-start | bytes 1114112 | tf_op jit(solution)/shard_map/all_gather | solution.py:191
  233.2 434.8 %reduce-scatter.2.cloned.1.call-start = ((), (), s32[]{:S(2)}) async-start(), calls=%async_computation.5 | async-start | bytes 2228224 | tf_op jit(solution)/shard_map/reduce_scatter | solution.py:192
  603.3 66.3 %copy-start.1 = (bf16[3,128,1,256]{3,1,2,0:T(8,128)(2,1)S(1)}, bf16[3,128,1,256]{3,1,2,0:T(8,128)(2,1)}, u32[]{:S(2)}) copy-start(bf16[3,128,1,256]{3,1,2,0:T(8,128)(2,1)} %param.26) | copy-start | bytes 589828
  (3 other events, 10.0 us)
Sparse Core Ops, SparseCore 0:
  9.1 67.9 all-gather.8
  79.0 52.1 all-gather.6
  144.1 34.2 all-gather.14
  232.7 297.6 all-gather.10
  532.7 45.5 all-gather.12
  607.1 60.7 reduce-scatter.1
